TPU v7x, 256 devices: a whole 4x4x8 slice. The times are simulated.
256 devices in a mesh: fsdp: 32 (over y, x, core), rep: 8 (over z).
Axes of the slice: x: 4, y: 4, z: 8, core: 2. Of those that a mesh axis runs over, the one named last changes fastest.
Arguments:
- tokens: bfloat16 [8, 4096, 2048], P('rep', 'fsdp'), may hold values from -6 to 6
- upstream: bfloat16 [8, 7168, 4096], P('rep', 'fsdp'), may hold values from -0.25 to 0.25
- weight: bfloat16 [2, 7168, 2048], P(None, 'fsdp'), may hold values from -0.125 to 0.125
- feedback: float32 [8, 2, 7168, 2048], P('rep', None, 'fsdp'), may hold values from -6 to 6
- momentum: float32 [2, 7168, 2048], P(None, 'fsdp', 'rep'), may hold values from -6 to 6
- right_factor: float32 [2, 7168, 64], P(None, 'fsdp'), may hold values from -6 to 6
Outputs:
- feedback_next: float32 [8, 2, 7168, 2048], P('rep', None, 'fsdp')
- momentum_next: float32 [2, 7168, 2048], P(None, 'fsdp', 'rep')
- weight_next: bfloat16 [2, 7168, 2048], P(None, 'fsdp', 'rep')
- right_next: float32 [2, 7168, 64], P(None, 'fsdp')
All inputs are finite; a program needn't handle non-finite values.
Results may differ from a plain program's by a relative error of at most 0.0023.
Values may be sent and summed in bfloat16 or wider, within the bound.
A program may use at most 128 MiB of HBM per device.

v0:
```python
import jax
import jax.numpy as jnp
from jax import lax
from jax.sharding import PartitionSpec as P

momentum_decay = 0.9
step_rate = 0.05
highest = lax.Precision.HIGHEST


def silu_pair(gate_pre):
    sigmoid = jax.nn.sigmoid(gate_pre)
    return (gate_pre * sigmoid, sigmoid * (1.0 + gate_pre * (1.0 - sigmoid)))


def solve_basis(factor, gram_matrix):
    lower_factor = jnp.linalg.cholesky(gram_matrix)
    return lax.linalg.triangular_solve(
        lower_factor, factor, left_side=False, lower=True, transpose_a=True
    )


def local_gram(factor):
    return jnp.einsum("kdr,kds->krs", factor, factor, precision=highest)


def per_device(tokens, upstream, weight, feedback, momentum, right_factor):
    own_rows = tokens[0]
    cotangents = upstream[0]
    contract_last = (((1,), (1,)), ((), ()))
    segment = lax.all_gather(own_rows, "fsdp", axis=0, tiled=True)
    cotangent_wide = cotangents.astype(jnp.float32)
    gate_pre = lax.dot_general(
        weight[0], segment, contract_last, preferred_element_type=jnp.float32
    )
    up_pre = lax.dot_general(weight[1], segment, contract_last, preferred_element_type=jnp.float32)
    activated, derivative = silu_pair(gate_pre)
    grad_gate = (cotangent_wide * up_pre * derivative).astype(jnp.bfloat16)
    grad_up = (cotangent_wide * activated).astype(jnp.bfloat16)
    term_gate = jnp.dot(grad_gate, segment, preferred_element_type=jnp.float32)
    term_up = jnp.dot(grad_up, segment, preferred_element_type=jnp.float32)
    gradient = jnp.stack([term_gate, term_up])
    delta = gradient + feedback[0]
    left_part = jnp.einsum("kfd,kfr->kdr", delta, right_factor, precision=highest)
    replicas = lax.axis_size("rep")
    left_mean = lax.psum(left_part, ("fsdp", "rep")) / replicas
    basis = solve_basis(left_mean, local_gram(left_mean))
    right_part = jnp.einsum("kfd,kdr->kfr", delta, basis, precision=highest)
    right_next = lax.psum(right_part, "rep") / replicas
    approx = jnp.einsum("kdr,kfr->kfd", basis, right_next, precision=highest)
    feedback_next = (delta - approx)[None]
    slab_cols = momentum.shape[2]
    slab_start = lax.axis_index("rep") * slab_cols
    approx_slab = lax.dynamic_slice_in_dim(approx, slab_start, slab_cols, 2)
    weight_slab = lax.dynamic_slice_in_dim(weight, slab_start, slab_cols, 2)
    momentum_next = momentum_decay * momentum + approx_slab
    weight_next = (weight_slab.astype(jnp.float32) - step_rate * momentum_next).astype(jnp.bfloat16)
    return (feedback_next, momentum_next, weight_next, right_next)


def solution(mesh):
    placed = (
        P("rep", "fsdp", None),
        P("rep", "fsdp", None),
        P(None, "fsdp", None),
        P("rep", None, "fsdp", None),
        P(None, "fsdp", "rep"),
        P(None, "fsdp", None),
    )
    return jax.shard_map(
        per_device,
        mesh=mesh,
        in_specs=placed,
        out_specs=(
            P("rep", None, "fsdp", None),
            P(None, "fsdp", "rep"),
            P(None, "fsdp", "rep"),
            P(None, "fsdp", None),
        ),
        check_vma=False,
    )
```

profile of v0, /device:TPU:2, one launch (start us, length us, event | category | flops | bytes accessed | tf_op | source)
XLA Modules:
  0.0 520.9 jit_solution(15495969798062645339)
XLA Ops:
  7.2 0.0 copy-start
  7.2 0.0 all-gather.3.cloned.1.call-start
  7.2 0.7 all-gather.3.cloned.1.call-update
  7.9 0.0 all-reduce.3.cloned.1.call-start
  8.0 83.1 %all-gather.3.cloned.1.call-done = bf16[1,4096,2048]{2,1,0:T(8,128)(2,1)} async-done(((bf16[1,128,2048]{2,1,0:T(8,128)(2,1)}), bf16[1,4096,2048]{2,1,0:T(8,128)(2,1)}) %all-gather.3.cloned.1.call-update) | async-done | bytes 16777232 | tf_op jit(solution)/shard_map/all_gather | solution.py:31
  91.1 13.0 %fusion.4 = f32[224,4096]{1,0:T(8,128)} fusion(bf16[1,4096,2048]{2,1,0:T(8,128)(2,1)} %all-gather.3.cloned.1.call-done, bf16[2,224,2048]{2,1,0:T(8,128)(2,1)} %param.8), kind=kOutput, calls=%fused_computation.4 | convolution fusion | flops 3758096384 | bytes 21364736 | tf_op jit(solution)/shard_map/dot_general | solution.py:33
  104.1 20.5 %fusion.25 = f32[1,224,2048]{2,1,0:T(8,128)S(1)} fusion(bf16[1,4096,2048]{2,1,0:T(8,128)(2,1)} %all-gather.3.cloned.1.call-done, f32[224,4096]{1,0:T(8,128)} %fusion.4, bf16[1,224,4096]{2,1,0:T(8,128)(2,1)} %param.7, bf16[2,224,2048]{2,1,0:T(8,128)(2,1)} %param.8), kind=kOutput, calls=%fused_computation.21 | convolution fusion | flops 7526285312 | bytes 41811968 | tf_op jit(solution)/shard_map/dot_general | solution.py:40
  124.7 0.0 copy-start.1
  124.7 9.7 %fusion.30 = f32[1,224,2048]{2,1,0:T(8,128)S(1)} fusion(bf16[1,4096,2048]{2,1,0:T(8,128)(2,1)} %all-gather.3.cloned.1.call-done, f32[224,4096]{1,0:T(8,128)} %fusion.4, bf16[1,224,4096]{2,1,0:T(8,128)(2,1)} %param.7), kind=kOutput, calls=%fused_computation.22 | convolution fusion | flops 3764518912 | bytes 24117248 | tf_op jit(solution)/shard_map/dot_general | solution.py:41
  134.4 0.0 copy-start.3
  134.4 1.2 copy-done.3
  135.7 0.0 copy-done
  135.7 0.0 copy-done.1
  135.7 3.6 fusion.57
  139.3 0.0 all-reduce.3.cloned.1.call-update
  139.3 0.2 all-reduce.5.cloned.1.call-start
  139.6 258.4 %all-reduce.3.cloned.1.call-done = f32[2,2048,64]{1,2,0:T(8,128)} async-done(((f32[2,2048,64]{1,2,0:T(8,128)}), f32[2,2048,64]{1,2,0:T(8,128)}) %all-reduce.3.cloned.1.call-update) | async-done | bytes 1048592 | tf_op jit(solution)/shard_map/psum | solution.py:46
  397.9 2.7 fusion.40
  400.6 0.1 copy.12
  400.7 11.7 %custom-call.7 = f32[2,64,64]{2,1,0:T(8,128)S(1)} custom-call(f32[2,64,64]{2,1,0:T(8,128)S(1)} %fusion.51), custom_call_target="Cholesky" | custom-call | tf_op jit(solution)/shard_map/jit(cholesky)/cholesky | solution.py:17
  412.5 0.1 compare_reduce_fusion
  412.6 0.1 select_bitcast_fusion
  412.7 9.8 %custom-call.8 = f32[2,1,64,64]{2,3,1,0:T(8,128)S(1)} custom-call(f32[2,1,64,64]{3,2,1,0:T(8,128)S(1)} %select_bitcast_fusion), custom_call_target="InvertDiagBlocksLowerTriangular" | custom-call | tf_op jit(solution)/shard_map/triangular_solve | solution.py:18
  422.5 2.3 fusion.38
  424.9 7.1 %fusion.56 = f32[2,224,64]{1,2,0:T(8,128)} fusion(f32[2,2048,64]{1,2,0:T(8,128)S(1)} %fusion.38, f32[1,224,2048]{2,1,0:T(8,128)} %copy-done.3, f32[1,224,2048]{2,1,0:T(8,128)S(1)} %fusion.25, f32[1,2,224,2048]{3,2,1,0:T(8,128)} %param.9), kind=kOutput, calls=%fused_computation.52 | convolution fusion | flops 706478080 | bytes 8503296 | tf_op jit(solution)/shard_map/kfd,kdr->kfr/dot_general | solution.py:48
  432.0 0.0 all-reduce.5.cloned.1.call-update
  432.0 71.5 %all-reduce.5.cloned.1.call-done = f32[2,224,64]{1,2,0:T(8,128)} async-done(((f32[2,224,64]{1,2,0:T(8,128)}), f32[2,224,64]{1,2,0:T(8,128)}) %all-reduce.5.cloned.1.call-update) | async-done | bytes 114704 | tf_op jit(solution)/shard_map/psum | solution.py:49
  503.5 0.0 copy-start.2
  503.5 1.1 broadcast_multiply_fusion
  504.5 0.0 copy-start.4
  504.5 3.1 fusion.58
  507.6 0.0 copy-done.2
  507.6 0.0 copy-start.5
  507.6 4.8 subtract_bitcast_fusion
  512.5 0.0 copy-done.4
  512.5 0.0 copy-done.5
  512.5 1.9 subtract_convert_fusion
  (4 shorter events, 0.1 us)
Async XLA Ops:
  7.2 128.5 %copy-start = (f32[2,224,64]{1,2,0:T(8,128)S(1)}, f32[2,224,64]{1,2,0:T(8,128)}, u32[]{:S(2)}) copy-start(f32[2,224,64]{1,2,0:T(8,128)} %param.11) | copy-start | bytes 344068
  7.2 83.9 %all-gather.3.cloned.1.call-start = ((), (), s32[]{:S(2)}) async-start(), calls=%async_computation.2 | async-start | bytes 17301504 | tf_op jit(solution)/shard_map/all_gather | solution.py:31
  7.9 390.0 %all-reduce.3.cloned.1.call-start = ((), (), s32[]{:S(2)}) async-start(), calls=%async_computation | async-start | bytes 2097152 | tf_op jit(solution)/shard_map/psum | solution.py:46
  124.7 11.0 %copy-start.1 = (f32[1,2,224,2048]{3,2,1,0:T(8,128)S(1)}, f32[1,2,224,2048]{3,2,1,0:T(8,128)}, u32[]{:S(2)}) copy-start(f32[1,2,224,2048]{3,2,1,0:T(8,128)} %param.9) | copy-start | bytes 11010052
  134.4 1.3 copy-start.3
  139.3 364.2 %all-reduce.5.cloned.1.call-start = ((), (), s32[]{:S(2)}) async-start(), calls=%async_computation.1 | async-start | bytes 262144 | tf_op jit(solution)/shard_map/psum | solution.py:49
  503.5 4.2 copy-start.2
  504.5 8.0 %copy-start.4 = (f32[2,224,64]{1,2,0:T(8,128)}, f32[2,224,64]{1,2,0:T(8,128)S(1)}, u32[]{:S(2)}) copy-start(f32[2,224,64]{1,2,0:T(8,128)S(1)} %broadcast_multiply_fusion) | copy-start | bytes 344068
  507.6 4.9 copy-start.5
Sparse Core Ops, SparseCore 0:
  10.5 80.4 all-gather.2
  139.4 258.4 all-reduce.2
  432.1 71.3 all-reduce.4
where the time goes:
time: 521 us
  waiting for transfers between devices  414 us (79%)
  matrix products  62.1 us (12%)
  other arithmetic  29.6 us (6%)
  between operations  13.9 us (3%)
    psum x1, waiting for transfers between devices, per_device(): left_mean = lax.psum(left_part, ('fsdp', 'rep')) / replicas  258 us
    all_gather x1, waiting for transfers between devices, per_device(): segment = lax.all_gather(own_rows, 'fsdp', axis=0, tiled=True)  83.1 us
    psum x1, waiting for transfers between devices, per_device(): right_next = lax.psum(right_part, 'rep') / replicas  71.5 us
    dot_general x1, matrix products, per_device(): term_gate = jnp.dot(grad_gate, segment, preferred_element_type=jnp.float32)  20.5 us
    dot_general x1, matrix products, per_device(): lax.dot_general(weight[0], segment, contract_last, preferred_element_type...  13 us
    another operation x4, other arithmetic, solve_basis(): lower_factor = jnp.linalg.cholesky(gram_matrix)  11.9 us
  transfers between devices with their start and end apart: 3, of which 3 were waited for; matrix products, arithmetic and copies ran while one was open for 0% of the time, Pallas kernels for 0%

commit v1 on v0

--- a/solution.py
+++ b/solution.py
@@ -2,6 +2,7 @@
 import jax.numpy as jnp
 from jax import lax
 from jax.sharding import PartitionSpec as P
+from jax.lax import psum
 
 momentum_decay = 0.9
 step_rate = 0.05
@@ -25,6 +26,11 @@
 
 
 def per_device(tokens, upstream, weight, feedback, momentum, right_factor):
+
+    def refer_set_up(arr):
+        raw_out = psum(psum(arr, "fsdp"), "rep")
+        return raw_out
+
     own_rows = tokens[0]
     cotangents = upstream[0]
     contract_last = (((1,), (1,)), ((), ()))
@@ -43,7 +49,7 @@
     delta = gradient + feedback[0]
     left_part = jnp.einsum("kfd,kfr->kdr", delta, right_factor, precision=highest)
     replicas = lax.axis_size("rep")
-    left_mean = lax.psum(left_part, ("fsdp", "rep")) / replicas
+    left_mean = refer_set_up(left_part) / replicas
     basis = solve_basis(left_mean, local_gram(left_mean))
     right_part = jnp.einsum("kfd,kdr->kfr", delta, basis, precision=highest)
     right_next = lax.psum(right_part, "rep") / replicas

time: 521 us -> 455 us (0.87)
  waiting for transfers between devices: 414 us -> 348 us
    psum x1 -> x2, waiting for transfers between devices: 258 us -> 193 us  [refer_set_up(): raw_out = psum(psum(arr, 'fsdp'), 'rep')]
  transfers between devices with their start and end apart: 3 -> 4, of which waited for: 3 -> 4; matrix products, arithmetic and copies ran while one was open for 0% -> 0% of each run, Pallas kernels for 0% -> 0%
where the time goes in v1:
time: 455 us
  waiting for transfers between devices  348 us (76%)
  matrix products  62.1 us (14%)
  other arithmetic  29.6 us (7%)
  between operations  13.9 us (3%)
    psum x2, waiting for transfers between devices, refer_set_up(): raw_out = psum(psum(arr, 'fsdp'), 'rep')  193 us
    all_gather x1, waiting for transfers between devices, per_device(): segment = lax.all_gather(own_rows, 'fsdp', axis=0, tiled=True)  83.1 us
    psum x1, waiting for transfers between devices, per_device(): right_next = lax.psum(right_part, 'rep') / replicas  71.1 us
    dot_general x1, matrix products, per_device(): term_gate = jnp.dot(grad_gate, segment, preferred_element_type=jnp.float32)  20.5 us
    dot_general x1, matrix products, per_device(): lax.dot_general(weight[0], segment, contract_last, preferred_element_type...  13 us
    another operation x4, other arithmetic, solve_basis(): lower_factor = jnp.linalg.cholesky(gram_matrix)  11.9 us
    another operation x3, other arithmetic, solve_basis(): lax.linalg.triangular_solve(lower_factor, factor, left_side=False, lower=...  9.92 us
    dot_general x1, matrix products, per_device(): term_up = jnp.dot(grad_up, segment, preferred_element_type=jnp.float32)  9.73 us
  transfers between devices with their start and end apart: 4, of which 4 were waited for; matrix products, arithmetic and copies ran while one was open for 0% of the time, Pallas kernels for 0%

profile of v1, /device:TPU:2, one launch (start us, length us, event | category | flops | bytes accessed | tf_op | source)
XLA Modules:
  0.0 455.2 jit_solution(7111119741998840525)
XLA Ops:
  7.2 0.0 copy-start
  7.2 0.0 all-gather.3.cloned.1.call-start
  7.2 0.7 all-gather.3.cloned.1.call-update
  7.9 0.0 all-reduce.4.cloned.1.call-start
  8.0 83.1 %all-gather.3.cloned.1.call-done = bf16[1,4096,2048]{2,1,0:T(8,128)(2,1)} async-done(((bf16[1,128,2048]{2,1,0:T(8,128)(2,1)}), bf16[1,4096,2048]{2,1,0:T(8,128)(2,1)}) %all-gather.3.cloned.1.call-update) | async-done | bytes 16777232 | tf_op jit(solution)/shard_map/all_gather | solution.py:37
  91.1 13.0 %fusion.4 = f32[224,4096]{1,0:T(8,128)} fusion(bf16[1,4096,2048]{2,1,0:T(8,128)(2,1)} %all-gather.3.cloned.1.call-done, bf16[2,224,2048]{2,1,0:T(8,128)(2,1)} %param.8), kind=kOutput, calls=%fused_computation.4 | convolution fusion | flops 3758096384 | bytes 21364736 | tf_op jit(solution)/shard_map/dot_general | solution.py:39
  104.1 20.5 %fusion.25 = f32[1,224,2048]{2,1,0:T(8,128)S(1)} fusion(bf16[1,4096,2048]{2,1,0:T(8,128)(2,1)} %all-gather.3.cloned.1.call-done, f32[224,4096]{1,0:T(8,128)} %fusion.4, bf16[1,224,4096]{2,1,0:T(8,128)(2,1)} %param.7, bf16[2,224,2048]{2,1,0:T(8,128)(2,1)} %param.8), kind=kOutput, calls=%fused_computation.21 | convolution fusion | flops 7526285312 | bytes 41811968 | tf_op jit(solution)/shard_map/dot_general | solution.py:46
  124.7 0.0 copy-start.1
  124.7 9.7 %fusion.30 = f32[1,224,2048]{2,1,0:T(8,128)S(1)} fusion(bf16[1,4096,2048]{2,1,0:T(8,128)(2,1)} %all-gather.3.cloned.1.call-done, f32[224,4096]{1,0:T(8,128)} %fusion.4, bf16[1,224,4096]{2,1,0:T(8,128)(2,1)} %param.7), kind=kOutput, calls=%fused_computation.22 | convolution fusion | flops 3764518912 | bytes 24117248 | tf_op jit(solution)/shard_map/dot_general | solution.py:47
  134.4 0.0 copy-start.3
  134.4 1.2 copy-done.3
  135.7 0.0 copy-done
  135.7 0.0 copy-done.1
  135.7 3.6 fusion.57
  139.3 0.0 all-reduce.4.cloned.1.call-update
  139.3 0.0 all-reduce.6.cloned.1.call-start
  139.3 114.6 %all-reduce.4.cloned.1.call-done = f32[2,2048,64]{1,2,0:T(8,128)} async-done(((f32[2,2048,64]{1,2,0:T(8,128)}), f32[2,2048,64]{1,2,0:T(8,128)}) %all-reduce.4.cloned.1.call-update) | async-done | bytes 1048592 | tf_op jit(solution)/shard_map/psum | solution.py:31
  253.9 0.0 all-reduce.6.cloned.1.call-update
  253.9 0.2 all-reduce.8.cloned.1.call-start
  254.2 78.4 %all-reduce.6.cloned.1.call-done = f32[2,2048,64]{1,2,0:T(8,128)} async-done(((f32[2,2048,64]{1,2,0:T(8,128)}), f32[2,2048,64]{1,2,0:T(8,128)}) %all-reduce.6.cloned.1.call-update) | async-done | bytes 1048592 | tf_op jit(solution)/shard_map/psum | solution.py:31
  332.6 2.7 fusion.40
  335.3 0.1 copy.12
  335.4 11.7 %custom-call.7 = f32[2,64,64]{2,1,0:T(8,128)S(1)} custom-call(f32[2,64,64]{2,1,0:T(8,128)S(1)} %fusion.51), custom_call_target="Cholesky" | custom-call | tf_op jit(solution)/shard_map/jit(cholesky)/cholesky | solution.py:18
  347.2 0.1 compare_reduce_fusion
  347.3 0.1 select_bitcast_fusion
  347.4 9.8 %custom-call.8 = f32[2,1,64,64]{2,3,1,0:T(8,128)S(1)} custom-call(f32[2,1,64,64]{3,2,1,0:T(8,128)S(1)} %select_bitcast_fusion), custom_call_target="InvertDiagBlocksLowerTriangular" | custom-call | tf_op jit(solution)/shard_map/triangular_solve | solution.py:19
  357.2 2.3 fusion.38
  359.6 7.1 %fusion.56 = f32[2,224,64]{1,2,0:T(8,128)} fusion(f32[2,2048,64]{1,2,0:T(8,128)S(1)} %fusion.38, f32[1,224,2048]{2,1,0:T(8,128)} %copy-done.3, f32[1,224,2048]{2,1,0:T(8,128)S(1)} %fusion.25, f32[1,2,224,2048]{3,2,1,0:T(8,128)} %param.9), kind=kOutput, calls=%fused_computation.52 | convolution fusion | flops 706478080 | bytes 8503296 | tf_op jit(solution)/shard_map/kfd,kdr->kfr/dot_general | solution.py:54
  366.7 0.0 all-reduce.8.cloned.1.call-update
  366.7 71.1 %all-reduce.8.cloned.1.call-done = f32[2,224,64]{1,2,0:T(8,128)} async-done(((f32[2,224,64]{1,2,0:T(8,128)}), f32[2,224,64]{1,2,0:T(8,128)}) %all-reduce.8.cloned.1.call-update) | async-done | bytes 114704 | tf_op jit(solution)/shard_map/psum | solution.py:55
  437.8 0.0 copy-start.2
  437.8 1.1 broadcast_multiply_fusion
  438.9 0.0 copy-start.4
  438.9 3.1 fusion.58
  442.0 0.0 copy-done.2
  442.0 0.0 copy-start.5
  442.0 4.8 %subtract_bitcast_fusion = f32[1,2,224,2048]{3,2,1,0:T(8,128)} fusion(f32[2,224,2048]{2,1,0:T(8,128)S(1)} %fusion.58, f32[1,2,224,2048]{3,2,1,0:T(8,128)S(1)} %copy-done.2, f32[1,224,2048]{2,1,0:T(8,128)} %copy-done.3, f32[1,224,2048]{2,1,0:T(8,128)S(1)} %fusion.25), kind=kLoop, calls=%fused_computation.15 | loop fusion | flops 2752512 | bytes 14680064 | tf_op jit(solution)/shard_map/broadcast_in_dim | solution.py:57
  446.8 0.0 copy-done.4
  446.8 0.0 copy-done.5
  446.8 1.9 subtract_convert_fusion
  (4 shorter events, 0.1 us)
Async XLA Ops:
  7.2 128.5 %copy-start = (f32[2,224,64]{1,2,0:T(8,128)S(1)}, f32[2,224,64]{1,2,0:T(8,128)}, u32[]{:S(2)}) copy-start(f32[2,224,64]{1,2,0:T(8,128)} %param.11) | copy-start | bytes 344068
  7.2 83.9 %all-gather.3.cloned.1.call-start = ((), (), s32[]{:S(2)}) async-start(), calls=%async_computation.3 | async-start | bytes 17301504 | tf_op jit(solution)/shard_map/all_gather | solution.py:37
  7.9 246.0 %all-reduce.4.cloned.1.call-start = ((), (), s32[]{:S(2)}) async-start(), calls=%async_computation | async-start | bytes 2097152 | tf_op jit(solution)/shard_map/psum | solution.py:31
  124.7 11.0 %copy-start.1 = (f32[1,2,224,2048]{3,2,1,0:T(8,128)S(1)}, f32[1,2,224,2048]{3,2,1,0:T(8,128)}, u32[]{:S(2)}) copy-start(f32[1,2,224,2048]{3,2,1,0:T(8,128)} %param.9) | copy-start | bytes 11010052
  134.4 1.3 copy-start.3
  139.3 193.3 %all-reduce.6.cloned.1.call-start = ((), (), s32[]{:S(2)}) async-start(), calls=%async_computation.1 | async-start | bytes 2097152 | tf_op jit(solution)/shard_map/psum | solution.py:31
  253.9 183.9 %all-reduce.8.cloned.1.call-start = ((), (), s32[]{:S(2)}) async-start(), calls=%async_computation.2 | async-start | bytes 262144 | tf_op jit(solution)/shard_map/psum | solution.py:55
  437.8 4.2 copy-start.2
  438.9 8.0 %copy-start.4 = (f32[2,224,64]{1,2,0:T(8,128)}, f32[2,224,64]{1,2,0:T(8,128)S(1)}, u32[]{:S(2)}) copy-start(f32[2,224,64]{1,2,0:T(8,128)S(1)} %broadcast_multiply_fusion) | copy-start | bytes 344068
  442.0 4.9 %copy-start.5 = (f32[2,224,256]{2,1,0:T(8,128)S(1)}, f32[2,224,256]{2,1,0:T(8,128)}, u32[]{:S(2)}) copy-start(f32[2,224,256]{2,1,0:T(8,128)} %param.10) | copy-start | bytes 1376260
Sparse Core Ops, SparseCore 0:
  10.5 80.4 all-gather.2
  139.4 114.4 all-reduce.3
  256.3 76.3 all-reduce.5
  366.8 70.9 all-reduce.7
